TPU v7x, 128 devices: a whole 4x4x4 slice. The times are simulated.
128 devices in a mesh: section: 2 (over core), blk: 16 (over y, x), mp: 4 (over z).
Axes of the slice: x: 4, y: 4, z: 4, core: 2. Of those that a mesh axis runs over, the one named last changes fastest.
Arguments:
- patches: bfloat16 [256, 5120], P('section'), may hold values from -6 to 6
- merge_gain: float32 [1280], replicated, may hold values from 0.25 to 1.75
- merge_first: bfloat16 [5120, 5120], P(None, ('blk', 'mp')), may hold values from -0.078125 to 0.078125
- merge_second: bfloat16 [5120, 4096], P(('blk', 'mp')), may hold values from -0.078125 to 0.078125
- text_embeds: bfloat16 [4, 1024, 4096], P(None, 'blk', 'mp'), may hold values from -7 to 14
- positions: int32 [256], replicated, may hold values from 0 to 4095, as said below
- segments: int32 [4096], replicated, may hold values from 0 to 2, never falling along the last dimension, each value on 1 to 2048 neighbouring positions
- norm_gain: float32 [2, 4096], P('section'), may hold values from 0.25 to 1.75
- query_weight: bfloat16 [2, 4096, 4096], P('section', 'blk', 'mp'), may hold values from -1 to 1
- keyval_weight: bfloat16 [2, 4096, 4, 2, 128], P('section', 'blk', 'mp'), may hold values from -1 to 1
- out_weight: bfloat16 [2, 4096, 4096], P('section', 'mp', 'blk'), may hold values from -0.09375 to 0.09375
Outputs:
- hidden: bfloat16 [2, 4, 1024, 4096], P('section', None, 'blk', 'mp')
Inputs may be any that keep to these rules, and one draw needn't show every extreme that they name: `positions`: distinct and increasing.
All inputs are finite; a program needn't handle non-finite values.
Results may differ from a plain program's by a relative error of at most 0.015.
Values may be sent and summed in bfloat16 or wider, within the bound.
No kernel may reach another device: no remote copies, remote signals or barrier semaphores. Data moves between devices by JAX's collectives and lax.ppermute only.
A program may use at most 128 MiB of HBM per device.

v0:
```python
import jax
import jax.numpy as jnp
from jax import lax
from jax.sharding import PartitionSpec as P

epsilon = 1e-06
rope_base = 1000000.0


def shifted(value, axis, by):
    size = lax.axis_size(axis)
    pairs = [(i, i + by) for i in range(size) if 0 <= i + by < size]
    return lax.ppermute(value, axis, pairs)


def rope_tables(where_at, head_size):
    steps_half = jnp.arange(head_size // 2).astype(jnp.float32)
    inverse = jnp.exp(-jnp.log(rope_base) * 2.0 * steps_half / head_size)
    angles = where_at.astype(jnp.float32)[:, None] * inverse[None, :]
    return (jnp.cos(angles), jnp.sin(angles))


def rotate(values, cosine, sine):
    half = values.shape[-1] // 2
    first = values[..., :half]
    second = values[..., half:]
    cosine = cosine[:, None, :]
    sine = sine[:, None, :]
    return jnp.concatenate(
        [first * cosine - second * sine, second * cosine + first * sine], axis=-1
    )


def local(
    patches,
    merge_gain,
    merge_first,
    merge_second,
    text_embeds,
    positions,
    segments,
    norm_gain,
    query_weight,
    keyval_weight,
    out_weight,
):
    count = patches.shape[0]
    width = merge_gain.shape[0]
    blocks = text_embeds.shape[0]
    rows_here = text_embeds.shape[1]
    slice_width = text_embeds.shape[2]
    seq_len = segments.shape[0]
    block_len = seq_len // blocks
    section_index = lax.axis_index("section")
    cycle_index = lax.axis_index("blk")
    model_index = lax.axis_index("mp")
    pieces = patches.astype(jnp.float32).reshape(count, -1, width)
    centered = pieces - jnp.mean(pieces, axis=-1, keepdims=True)
    variance = jnp.mean(centered * centered, axis=-1, keepdims=True)
    normed = (
        (centered * lax.rsqrt(variance + epsilon) * merge_gain)
        .reshape(count, -1)
        .astype(jnp.bfloat16)
    )
    inner = jax.nn.gelu(
        jnp.dot(normed, merge_first, preferred_element_type=jnp.float32), approximate=False
    ).astype(jnp.bfloat16)
    partial_merge = jnp.dot(inner, merge_second, preferred_element_type=jnp.float32)
    merged_full = lax.psum(partial_merge, ("blk", "mp")).astype(jnp.bfloat16)
    merged_mine = lax.dynamic_slice_in_dim(merged_full, model_index * slice_width, slice_width, 1)
    visual_all = lax.all_gather(merged_mine, "section", axis=0, tiled=True)
    query_full, keyval_full, out_full = (
        lax.all_gather(query_weight, "blk", axis=1, tiled=True),
        lax.all_gather(keyval_weight, "blk", axis=1, tiled=True),
        lax.all_gather(out_weight, "blk", axis=2, tiled=True),
    )
    query_full = query_full[0]
    kv_heads = keyval_full.shape[2]
    head_size = keyval_full.shape[4]
    keyval_full = keyval_full[0].reshape(keyval_full.shape[1], -1)
    out_full = out_full[0]
    gain_here = norm_gain[0]
    group = query_full.shape[1] // (kv_heads * head_size)
    scale = 1.0 / head_size**0.5
    key_where = jnp.arange(seq_len)
    ticks = blocks + lax.axis_size("section") - 1
    zero_index = jnp.zeros((), jnp.int32)
    held = jnp.zeros((rows_here, slice_width), jnp.bfloat16)
    cache_keys = jnp.zeros((seq_len, kv_heads, head_size), jnp.bfloat16)
    cache_values = jnp.zeros((seq_len, kv_heads, head_size), jnp.bfloat16)
    outputs = jnp.zeros((blocks, rows_here, slice_width), jnp.bfloat16)
    for tick_now in range(ticks):
        bound = min(tick_now + 1, blocks) * block_len
        block_now = tick_now - section_index
        active = (block_now >= 0) & (block_now < blocks)
        block_safe = jnp.clip(block_now, 0, blocks - 1)
        row_where = block_safe * block_len + cycle_index * rows_here + jnp.arange(rows_here)
        is_visual = positions[None, :] == row_where[:, None]
        picked = jnp.dot(
            is_visual.astype(jnp.bfloat16), visual_all, preferred_element_type=jnp.float32
        ).astype(jnp.bfloat16)
        text_rows = lax.dynamic_index_in_dim(text_embeds, block_safe, 0, keepdims=False)
        embedded = jnp.where(jnp.any(is_visual, axis=1)[:, None], picked, text_rows)
        incoming = jnp.where(section_index == 0, embedded, held)
        features = lax.all_gather(incoming, "mp", axis=1, tiled=True)
        feat_f = features.astype(jnp.float32)
        normx = (
            feat_f
            * lax.rsqrt(jnp.mean(feat_f * feat_f, axis=-1, keepdims=True) + epsilon)
            * gain_here
        ).astype(jnp.bfloat16)
        cosine, sine = rope_tables(row_where, head_size)
        query = jnp.dot(normx, query_full, preferred_element_type=jnp.float32).reshape(
            rows_here, -1, head_size
        )
        query = (
            rotate(query, cosine, sine)
            .astype(jnp.bfloat16)
            .reshape(rows_here, kv_heads, group, head_size)
        )
        keyval = jnp.dot(normx, keyval_full, preferred_element_type=jnp.float32).reshape(
            rows_here, kv_heads, 2, head_size
        )
        new_keys = rotate(keyval[:, :, 0, :], cosine, sine).astype(jnp.bfloat16)
        new_values = keyval[:, :, 1, :].astype(jnp.bfloat16)
        block_keys, block_values = (
            lax.all_gather(new_keys, "blk", axis=0, tiled=True),
            lax.all_gather(new_values, "blk", axis=0, tiled=True),
        )
        start = block_safe * block_len
        cache_keys = jnp.where(
            active,
            lax.dynamic_update_slice(cache_keys, block_keys, (start, zero_index, zero_index)),
            cache_keys,
        )
        cache_values = jnp.where(
            active,
            lax.dynamic_update_slice(cache_values, block_values, (start, zero_index, zero_index)),
            cache_values,
        )
        keys_seen = cache_keys[:bound]
        values_seen = cache_values[:bound]
        scores = (
            jnp.einsum("qkgd,skd->kgqs", query, keys_seen, preferred_element_type=jnp.float32)
            * scale
        )
        row_segments = jnp.take(segments, row_where)
        allowed = (key_where[None, :bound] <= row_where[:, None]) & (
            segments[None, :bound] == row_segments[:, None]
        )
        scores = jnp.where(allowed[None, None], scores, -jnp.inf)
        top = jnp.max(scores, axis=-1, keepdims=True)
        expo = jnp.exp(scores - top)
        probs = (expo / jnp.sum(expo, axis=-1, keepdims=True)).astype(jnp.bfloat16)
        attended = jnp.einsum(
            "kgqs,skd->qkgd", probs, values_seen, preferred_element_type=jnp.float32
        )
        attended = attended.reshape(rows_here, -1).astype(jnp.bfloat16)
        term = jnp.dot(attended, out_full, preferred_element_type=jnp.float32)
        summed = lax.psum_scatter(
            term.astype(jnp.bfloat16), "mp", scatter_dimension=1, tiled=True
        ).astype(jnp.float32)
        result = (incoming.astype(jnp.float32) + summed).astype(jnp.bfloat16)
        outputs = jnp.where(
            active,
            lax.dynamic_update_slice(outputs, result[None], (block_safe, zero_index, zero_index)),
            outputs,
        )
        held = shifted(result, "section", 1)
    return outputs[None]


def solution(mesh):
    return jax.shard_map(
        local,
        mesh=mesh,
        in_specs=(
            P("section", None),
            P(),
            P(None, ("blk", "mp")),
            P(("blk", "mp"), None),
            P(None, "blk", "mp"),
            P(),
            P(),
            P("section", None),
            P("section", "blk", "mp"),
            P("section", "blk", "mp", None, None),
            P("section", "mp", "blk"),
        ),
        out_specs=P("section", None, "blk", "mp"),
        check_vma=False,
    )
```

profile of v0, /device:TPU:0, one launch (start us, length us, event | category | flops | bytes accessed | tf_op | source)
XLA Modules:
  0.0 948.9 jit_solution(6913599249277682439)
XLA Ops:
  23.5 383.3 %all-reduce.1 = bf16[128,4096]{1,0:T(8,128)(2,1)S(1)} all-reduce(f32[128,4096]{1,0:T(8,128)} %fusion.210), channel_id=1, replica_groups=mesh['section'=2,'blk'=16,'mp'=4] {'blk','mp'}, use_global_device_ids=true, to_apply=%region_3.4 | all-reduce | flops 524288 | bytes 3145728 | tf_op jit(solution)/shard_map/psum | solution.py:69
  411.0 13.4 %all_gather.58 = bf16[64,4096]{1,0:T(8,128)(2,1)S(1)} all-gather(bf16[64,1024]{1,0:T(8,128)(2,1)S(1)} %fusion.63), channel_id=1, replica_groups=mesh['section'=2,'blk'=16,'mp'=4] {'mp'}, dimensions={1}, use_global_device_ids=true | all-gather | bytes 655360 | tf_op jit(solution)/shard_map/all_gather | solution.py:105
  432.0 20.7 %all_gather.61 = bf16[1024,1,128]{2,0,1:T(8,128)(2,1)S(1)} all-gather(bf16[64,1,128]{2,0,1:T(8,128)(2,1)S(1)} %pad_maximum_fusion), channel_id=1, replica_groups=mesh['section'=2,'blk'=16,'mp'=4] {'blk'}, dimensions={0}, use_global_device_ids=true | all-gather | bytes 278528 | tf_op jit(solution)/shard_map/all_gather | solution.py:127
  452.7 24.1 %all-gather = bf16[1024,1,1,128]{3,0,2,1:T(8,128)(2,1)S(1)} all-gather(bf16[64,1,1,128]{3,0,2,1:T(8,128)(2,1)S(1)} %slice.285), channel_id=2, replica_groups=mesh['section'=2,'blk'=16,'mp'=4] {'blk'}, dimensions={0}, use_global_device_ids=true | all-gather | bytes 278528 | tf_op jit(solution)/shard_map/all_gather | solution.py:128
  480.5 11.8 %copy.31 = bf16[1024,4096]{1,0:T(8,128)(2,1)} copy(bf16[1024,4096]{0,1:T(8,128)(2,1)} %bitcast.333) | data formatting | bytes 16777216 | tf_op jit(solution)/shard_map/dot_general | solution.py:113
  511.2 15.4 %reduce-scatter.6.cloned.1.call-done = bf16[64,1024]{1,0:T(8,128)(2,1)} async-done(((bf16[64,4096]{1,0:T(8,128)(2,1)}), bf16[64,1024]{1,0:T(8,128)(2,1)}) %reduce-scatter.6.cloned.1.call-update) | async-done | bytes 131088 | tf_op jit(solution)/shard_map/reduce_scatter | solution.py:160
  531.9 13.5 %all_gather.64 = bf16[64,4096]{1,0:T(8,128)(2,1)S(1)} all-gather(bf16[64,1024]{1,0:T(8,128)(2,1)S(1)} %fusion.65), channel_id=1, replica_groups=mesh['section'=2,'blk'=16,'mp'=4] {'mp'}, dimensions={1}, use_global_device_ids=true | all-gather | bytes 655360 | tf_op jit(solution)/shard_map/all_gather | solution.py:105
  552.6 23.8 %all-gather.1 = bf16[1024,1,1,128]{3,0,2,1:T(8,128)(2,1)S(1)} all-gather(bf16[64,1,1,128]{3,0,2,1:T(8,128)(2,1)S(1)} %slice.284), channel_id=3, replica_groups=mesh['section'=2,'blk'=16,'mp'=4] {'blk'}, dimensions={0}, use_global_device_ids=true | all-gather | bytes 278528 | tf_op jit(solution)/shard_map/all_gather | solution.py:128
  576.7 23.3 %all_gather.66 = bf16[1024,1,128]{2,0,1:T(8,128)(2,1)S(1)} all-gather(bf16[64,1,128]{2,0,1:T(8,128)(2,1)S(1)} %pad_maximum_fusion.1), channel_id=1, replica_groups=mesh['section'=2,'blk'=16,'mp'=4] {'blk'}, dimensions={0}, use_global_device_ids=true | all-gather | bytes 278528 | tf_op jit(solution)/shard_map/all_gather | solution.py:127
  616.2 14.5 %reduce-scatter.8.cloned.1.call-done = bf16[64,1024]{1,0:T(8,128)(2,1)} async-done(((bf16[64,4096]{1,0:T(8,128)(2,1)}), bf16[64,1024]{1,0:T(8,128)(2,1)}) %reduce-scatter.8.cloned.1.call-update) | async-done | bytes 131088 | tf_op jit(solution)/shard_map/reduce_scatter | solution.py:160
  633.9 13.5 %all_gather.67 = bf16[64,4096]{1,0:T(8,128)(2,1)S(1)} all-gather(bf16[64,1024]{1,0:T(8,128)(2,1)S(1)} %broadcast_select_fusion.2), channel_id=1, replica_groups=mesh['section'=2,'blk'=16,'mp'=4] {'mp'}, dimensions={1}, use_global_device_ids=true | all-gather | bytes 655360 | tf_op jit(solution)/shard_map/all_gather | solution.py:105
  648.5 6.1 fusion.131
  654.6 23.8 %all-gather.2 = bf16[1024,1,1,128]{3,0,2,1:T(8,128)(2,1)S(1)} all-gather(bf16[64,1,1,128]{3,0,2,1:T(8,128)(2,1)S(1)} %slice.283), channel_id=4, replica_groups=mesh['section'=2,'blk'=16,'mp'=4] {'blk'}, dimensions={0}, use_global_device_ids=true | all-gather | bytes 278528 | tf_op jit(solution)/shard_map/all_gather | solution.py:128
  678.7 23.4 %all_gather.69 = bf16[1024,1,128]{2,0,1:T(8,128)(2,1)S(1)} all-gather(bf16[64,1,128]{2,0,1:T(8,128)(2,1)S(1)} %pad_maximum_fusion.2), channel_id=1, replica_groups=mesh['section'=2,'blk'=16,'mp'=4] {'blk'}, dimensions={0}, use_global_device_ids=true | all-gather | bytes 278528 | tf_op jit(solution)/shard_map/all_gather | solution.py:127
  715.8 17.7 %reduce-scatter.10.cloned.1.call-done = bf16[64,1024]{1,0:T(8,128)(2,1)} async-done(((bf16[64,4096]{1,0:T(8,128)(2,1)}), bf16[64,1024]{1,0:T(8,128)(2,1)}) %reduce-scatter.10.cloned.1.call-update) | async-done | bytes 131088 | tf_op jit(solution)/shard_map/reduce_scatter | solution.py:160
  737.7 13.4 %all_gather.70 = bf16[64,4096]{1,0:T(8,128)(2,1)S(1)} all-gather(bf16[64,1024]{1,0:T(8,128)(2,1)S(1)} %broadcast_select_fusion.1), channel_id=1, replica_groups=mesh['section'=2,'blk'=16,'mp'=4] {'mp'}, dimensions={1}, use_global_device_ids=true | all-gather | bytes 655360 | tf_op jit(solution)/shard_map/all_gather | solution.py:105
  752.1 6.1 fusion.134
  758.2 23.8 %all-gather.3 = bf16[1024,1,1,128]{3,0,2,1:T(8,128)(2,1)S(1)} all-gather(bf16[64,1,1,128]{3,0,2,1:T(8,128)(2,1)S(1)} %slice.282), channel_id=5, replica_groups=mesh['section'=2,'blk'=16,'mp'=4] {'blk'}, dimensions={0}, use_global_device_ids=true | all-gather | bytes 278528 | tf_op jit(solution)/shard_map/all_gather | solution.py:128
  782.3 23.2 %all_gather.72 = bf16[1024,1,128]{2,0,1:T(8,128)(2,1)S(1)} all-gather(bf16[64,1,128]{2,0,1:T(8,128)(2,1)S(1)} %pad_maximum_fusion.3), channel_id=1, replica_groups=mesh['section'=2,'blk'=16,'mp'=4] {'blk'}, dimensions={0}, use_global_device_ids=true | all-gather | bytes 278528 | tf_op jit(solution)/shard_map/all_gather | solution.py:127
  818.7 18.8 %reduce-scatter.12.cloned.1.call-done = bf16[64,1024]{1,0:T(8,128)(2,1)} async-done(((bf16[64,4096]{1,0:T(8,128)(2,1)}), bf16[64,1024]{1,0:T(8,128)(2,1)}) %reduce-scatter.12.cloned.1.call-update) | async-done | bytes 131088 | tf_op jit(solution)/shard_map/reduce_scatter | solution.py:160
  844.1 12.8 %all_gather.73 = bf16[64,4096]{1,0:T(8,128)(2,1)S(1)} all-gather(bf16[64,1024]{1,0:T(8,128)(2,1)S(1)} %broadcast_select_fusion), channel_id=1, replica_groups=mesh['section'=2,'blk'=16,'mp'=4] {'mp'}, dimensions={1}, use_global_device_ids=true | all-gather | bytes 655360 | tf_op jit(solution)/shard_map/all_gather | solution.py:105
  864.0 23.8 %all-gather.4 = bf16[1024,1,1,128]{3,0,2,1:T(8,128)(2,1)S(1)} all-gather(bf16[64,1,1,128]{3,0,2,1:T(8,128)(2,1)S(1)} %slice.281), channel_id=6, replica_groups=mesh['section'=2,'blk'=16,'mp'=4] {'blk'}, dimensions={0}, use_global_device_ids=true | all-gather | bytes 278528 | tf_op jit(solution)/shard_map/all_gather | solution.py:128
  888.0 23.3 %all_gather.75 = bf16[1024,1,128]{2,0,1:T(8,128)(2,1)S(1)} all-gather(bf16[64,1,128]{2,0,1:T(8,128)(2,1)S(1)} %pad_maximum_fusion.4), channel_id=1, replica_groups=mesh['section'=2,'blk'=16,'mp'=4] {'blk'}, dimensions={0}, use_global_device_ids=true | all-gather | bytes 278528 | tf_op jit(solution)/shard_map/all_gather | solution.py:127
  922.1 18.1 %reduce-scatter.14.cloned.1.call-done = bf16[64,1024]{1,0:T(8,128)(2,1)} async-done(((bf16[64,4096]{1,0:T(8,128)(2,1)}), bf16[64,1024]{1,0:T(8,128)(2,1)}) %reduce-scatter.14.cloned.1.call-update) | async-done | bytes 131088 | tf_op jit(solution)/shard_map/reduce_scatter | solution.py:160
  (316 shorter events, 142.5 us)
Async XLA Ops:
  6.5 419.6 %all-gather.9.cloned.1.call-start = ((), (), s32[]{:S(2)}) async-start(), calls=%async_computation.5 | async-start | bytes 2228224 | tf_op jit(solution)/shard_map/all_gather | solution.py:74
  7.3 473.2 %all-gather.11.cloned.1.call-start = ((), (), s32[]{:S(2)}) async-start(), calls=%async_computation.6 | async-start | bytes 8912896 | tf_op jit(solution)/shard_map/all_gather | solution.py:73
  8.0 494.1 %all-gather.13.cloned.1.call-start = ((), (), s32[]{:S(2)}) async-start(), calls=%async_computation.7 | async-start | bytes 8912896 | tf_op jit(solution)/shard_map/all_gather | solution.py:75
  8.7 517.9 %reduce-scatter.6.cloned.1.call-start = ((), (), s32[]{:S(2)}) async-start(), calls=%async_computation.8 | async-start | bytes 655360 | tf_op jit(solution)/shard_map/reduce_scatter | solution.py:160
  21.4 385.4 %copy-start.25 = (s32[256]{0:T(256)S(1)}, s32[256]{0:T(256)}, u32[]{:S(2)}) copy-start(s32[256]{0:T(256)} %param.18) | copy-start | bytes 3076
  21.4 403.2 %slice-start.8 = ((s32[4096]{0:T(1024)}), s32[1024]{0:T(1024)S(1)}, s32[]{:S(2)}) async-start(s32[4096]{0:T(1024)} %param.19), calls=%async_computation.21 | async-start | bytes 8192 | tf_op jit(solution)/shard_map/slice | solution.py:149
  21.4 404.6 %copy-start.46 = (f32[64]{0:T(128)}, f32[64]{0:T(128)S(1)}, u32[]{:S(2)}) copy-start(f32[64]{0:T(128)S(1)} %get-tuple-element.74) | copy-start | bytes 772
  22.2 554.2 %copy-start.26 = (f32[64]{0:T(128)}, f32[64]{0:T(128)S(1)}, u32[]{:S(2)}) copy-start(f32[64]{0:T(128)S(1)} %multiply_exponential_fusion) | copy-start | bytes 772
  22.2 384.6 %copy-start.44 = (s32[64]{0:T(128)}, s32[64]{0:T(128)S(1)}, u32[]{:S(2)}) copy-start(s32[64]{0:T(128)S(1)} %iota_add_fusion.5) | copy-start | bytes 772
  22.3 384.5 %copy-start.29 = (s32[64]{0:T(128)}, s32[64]{0:T(128)S(1)}, u32[]{:S(2)}) copy-start(s32[64]{0:T(128)S(1)} %get-tuple-element.77) | copy-start | bytes 772
  22.3 403.8 %copy-start.40 = (f32[64]{0:T(128)}, f32[64]{0:T(128)S(1)}, u32[]{:S(2)}) copy-start(f32[64]{0:T(128)S(1)} %get-tuple-element.80) | copy-start | bytes 772
  22.3 403.8 %copy-start.42 = (f32[64]{0:T(128)}, f32[64]{0:T(128)S(1)}, u32[]{:S(2)}) copy-start(f32[64]{0:T(128)S(1)} %get-tuple-element.79) | copy-start | bytes 772
  22.3 384.5 %copy-start.32 = (s32[64]{0:T(128)}, s32[64]{0:T(128)S(1)}, u32[]{:S(2)}) copy-start(s32[64]{0:T(128)S(1)} %get-tuple-element.75) | copy-start | bytes 772
  22.3 384.5 %copy-start.34 = (s32[64]{0:T(128)}, s32[64]{0:T(128)S(1)}, u32[]{:S(2)}) copy-start(s32[64]{0:T(128)S(1)} %get-tuple-element.76) | copy-start | bytes 772
  22.3 403.7 %copy-start.36 = (f32[64]{0:T(128)}, f32[64]{0:T(128)S(1)}, u32[]{:S(2)}) copy-start(f32[64]{0:T(128)S(1)} %get-tuple-element.82) | copy-start | bytes 772
  22.4 403.7 %copy-start.38 = (f32[64]{0:T(128)}, f32[64]{0:T(128)S(1)}, u32[]{:S(2)}) copy-start(f32[64]{0:T(128)S(1)} %get-tuple-element.81) | copy-start | bytes 772
  508.0 122.6 %reduce-scatter.8.cloned.1.call-start = ((), (), s32[]{:S(2)}) async-start(), calls=%async_computation.9 | async-start | bytes 655360 | tf_op jit(solution)/shard_map/reduce_scatter | solution.py:160
  527.7 2.4 collective-permute-start
  611.8 121.7 %reduce-scatter.10.cloned.1.call-start = ((), (), s32[]{:S(2)}) async-start(), calls=%async_computation.10 | async-start | bytes 655360 | tf_op jit(solution)/shard_map/reduce_scatter | solution.py:160
  631.6 2.3 collective-permute-start.1
  714.5 122.9 %reduce-scatter.12.cloned.1.call-start = ((), (), s32[]{:S(2)}) async-start(), calls=%async_computation.11 | async-start | bytes 655360 | tf_op jit(solution)/shard_map/reduce_scatter | solution.py:160
  734.5 2.5 collective-permute-start.2
  818.6 121.5 %reduce-scatter.14.cloned.1.call-start = ((), (), s32[]{:S(2)}) async-start(), calls=%async_computation.12 | async-start | bytes 655360 | tf_op jit(solution)/shard_map/reduce_scatter | solution.py:160
  838.5 4.9 collective-permute-start.3
  (58 other events, 1124.9 us)
Sparse Core Ops, SparseCore 0:
  9.5 47.7 all-gather.8
  59.5 74.0 all-gather.10
  135.7 81.8 all-gather.12
  508.1 18.4 reduce-scatter.5
  611.9 18.7 reduce-scatter.7
  714.6 18.8 reduce-scatter.9
  818.8 18.6 reduce-scatter.11
  921.4 18.7 reduce-scatter.13
where the time goes:
time: 957 us; the launch traced here: 949 us
  blocking collectives  685 us (72%)
  waiting for transfers between devices  87 us (9%)
  matrix products  81.5 us (9%)
  other arithmetic  37.5 us (4%)
  local copies, waits for them, and re-layouts  37.3 us (4%)
  between operations  15.1 us (2%)
    psum x1, blocking collectives, local(): merged_full = lax.psum(partial_merge, ('blk', 'mp')).astype(jnp.bfloat16)  383 us
    all_gather x5, blocking collectives, local(): lax.all_gather(new_values, 'blk', axis=0, tiled=True)  119 us
    all_gather x5, blocking collectives, local(): lax.all_gather(new_keys, 'blk', axis=0, tiled=True)  114 us
    reduce_scatter x5, waiting for transfers between devices, local(): lax.psum_scatter(term.astype(jnp.bfloat16), 'mp', scatter_dimension=1, ti...  84.4 us
    all_gather x5, blocking collectives, local(): features = lax.all_gather(incoming, 'mp', axis=1, tiled=True)  66.5 us
    dot_general x5, matrix products, local(): jnp.dot(normx, query_full, preferred_element_type=jnp.float32)  30.4 us
  transfers between devices with their start and end apart: 12, of which 6 were waited for; matrix products, arithmetic and copies ran while one was open for 7% of the time, Pallas kernels for 0%

commit v1 on v0

--- a/solution.py
+++ b/solution.py
@@ -5,6 +5,19 @@
 
 epsilon = 1e-06
 rope_base = 1000000.0
+
+
+def gather_around(x, axis, dim):
+    ways = lax.axis_size(axis)
+    up = [(d, (d + 1) % ways) for d in range(ways)]
+    down = [(d, (d - 1) % ways) for d in range(ways)]
+    earlier, later = ([x], [x])
+    for _ in range(ways // 2):
+        earlier.append(lax.ppermute(earlier[-1], axis, up))
+    for _ in range((ways - 1) // 2):
+        later.append(lax.ppermute(later[-1], axis, down))
+    line = jnp.concatenate([*earlier[::-1], *later[1:]], axis=dim)
+    return jnp.roll(line, (lax.axis_index(axis) - ways // 2) * x.shape[dim], axis=dim)
 
 
 def shifted(value, axis, by):
@@ -125,7 +138,7 @@
         new_values = keyval[:, :, 1, :].astype(jnp.bfloat16)
         block_keys, block_values = (
             lax.all_gather(new_keys, "blk", axis=0, tiled=True),
-            lax.all_gather(new_values, "blk", axis=0, tiled=True),
+            gather_around(new_values, "blk", 0),
         )
         start = block_safe * block_len
         cache_keys = jnp.where(

time: 957 us -> 1100 us (1.15)
  starting transfers between devices: 5.47 us -> 185 us
  blocking collectives: 685 us -> 569 us
  waiting for transfers between devices: 87 us -> 158 us
    ppermute x0 -> x75, starting transfers between devices: none -> 179 us  [the longest x35 172 us: gather_around(): later.append(lax.ppermute(later[-1], axis, down))]
    all_gather x5 -> x0, blocking collectives: 119 us -> none  [local(): lax.all_gather(new_values, 'blk', axis=0, tiled=True)]
    ppermute x0 -> x75, waiting for transfers between devices: none -> 58.7 us  [the longest x40 50.7 us: gather_around(): earlier.append(lax.ppermute(earlier[-1], axis, up))]
    reduce_scatter x5, waiting for transfers between devices: 84.4 us -> 96.5 us  [local(): lax.psum_scatter(term.astype(jnp.bfloat16), 'mp', scatter_dimension=1, ti...]
  transfers between devices with their start and end apart: 12 -> 87, of which waited for: 6 -> 35; matrix products, arithmetic and copies ran while one was open for 7% -> 11% of each run, Pallas kernels for 0% -> 0%
where the time goes in v1:
time: 1100 us; the launch traced here: 1090 us
  blocking collectives  569 us (52%)
  starting transfers between devices  185 us (17%)
  waiting for transfers between devices  158 us (14%)
  matrix products  81.1 us (7%)
  other arithmetic  43.1 us (4%)
  local copies, waits for them, and re-layouts  39.4 us (4%)
  between operations  15.6 us (1%)
    psum x1, blocking collectives, local(): merged_full = lax.psum(partial_merge, ('blk', 'mp')).astype(jnp.bfloat16)  383 us
    ppermute x35, starting transfers between devices, gather_around(): later.append(lax.ppermute(later[-1], axis, down))  172 us
    all_gather x5, blocking collectives, local(): lax.all_gather(new_keys, 'blk', axis=0, tiled=True)  117 us
    reduce_scatter x5, waiting for transfers between devices, local(): lax.psum_scatter(term.astype(jnp.bfloat16), 'mp', scatter_dimension=1, ti...  96.5 us
    all_gather x5, blocking collectives, local(): features = lax.all_gather(incoming, 'mp', axis=1, tiled=True)  67 us
    ppermute x40, waiting for transfers between devices, gather_around(): earlier.append(lax.ppermute(earlier[-1], axis, up))  50.7 us
    dot_general x5, matrix products, local(): jnp.dot(normx, query_full, preferred_element_type=jnp.float32)  30.3 us
  transfers between devices with their start and end apart: 87, of which 35 were waited for; matrix products, arithmetic and copies ran while one was open for 11% of the time, Pallas kernels for 0%

profile of v1, /device:TPU:0, one launch (start us, length us, event | category | flops | bytes accessed | tf_op | source)
XLA Modules:
  0.0 1091.2 jit_solution(5622180455597975725)
XLA Ops:
  22.4 383.3 %all-reduce.1 = bf16[128,4096]{1,0:T(8,128)(2,1)S(1)} all-reduce(f32[128,4096]{1,0:T(8,128)} %fusion.223), channel_id=1, replica_groups=mesh['section'=2,'blk'=16,'mp'=4] {'blk','mp'}, use_global_device_ids=true, to_apply=%region_3.4 | all-reduce | flops 524288 | bytes 3145728 | tf_op jit(solution)/shard_map/psum | solution.py:82
  410.0 13.5 %all_gather.43 = bf16[64,4096]{1,0:T(8,128)(2,1)S(1)} all-gather(bf16[64,1024]{1,0:T(8,128)(2,1)S(1)} %fusion.63), channel_id=1, replica_groups=mesh['section'=2,'blk'=16,'mp'=4] {'mp'}, dimensions={1}, use_global_device_ids=true | all-gather | bytes 655360 | tf_op jit(solution)/shard_map/all_gather | solution.py:118
  431.6 6.3 collective-permute-done
  473.3 23.4 %all_gather.45 = bf16[1024,1,128]{2,0,1:T(8,128)(2,1)S(1)} all-gather(bf16[64,1,128]{2,0,1:T(8,128)(2,1)S(1)} %pad_maximum_fusion), channel_id=1, replica_groups=mesh['section'=2,'blk'=16,'mp'=4] {'blk'}, dimensions={0}, use_global_device_ids=true | all-gather | bytes 278528 | tf_op jit(solution)/shard_map/all_gather | solution.py:140
  512.4 11.4 %copy.31 = bf16[1024,4096]{1,0:T(8,128)(2,1)} copy(bf16[1024,4096]{0,1:T(8,128)(2,1)} %bitcast.337) | data formatting | bytes 16777216 | tf_op jit(solution)/shard_map/dot_general | solution.py:126
  523.8 6.1 fusion.125
  542.7 16.8 %reduce-scatter.6.cloned.1.call-done = bf16[64,1024]{1,0:T(8,128)(2,1)} async-done(((bf16[64,4096]{1,0:T(8,128)(2,1)}), bf16[64,1024]{1,0:T(8,128)(2,1)}) %reduce-scatter.6.cloned.1.call-update) | async-done | bytes 131088 | tf_op jit(solution)/shard_map/reduce_scatter | solution.py:173
  564.9 13.4 %all_gather.48 = bf16[64,4096]{1,0:T(8,128)(2,1)S(1)} all-gather(bf16[64,1024]{1,0:T(8,128)(2,1)S(1)} %fusion.65), channel_id=1, replica_groups=mesh['section'=2,'blk'=16,'mp'=4] {'mp'}, dimensions={1}, use_global_device_ids=true | all-gather | bytes 655360 | tf_op jit(solution)/shard_map/all_gather | solution.py:118
  591.3 7.0 collective-permute-done.17
  612.5 23.4 %all_gather.49 = bf16[1024,1,128]{2,0,1:T(8,128)(2,1)S(1)} all-gather(bf16[64,1,128]{2,0,1:T(8,128)(2,1)S(1)} %pad_maximum_fusion.1), channel_id=1, replica_groups=mesh['section'=2,'blk'=16,'mp'=4] {'blk'}, dimensions={0}, use_global_device_ids=true | all-gather | bytes 278528 | tf_op jit(solution)/shard_map/all_gather | solution.py:140
  673.9 17.2 %reduce-scatter.8.cloned.1.call-done = bf16[64,1024]{1,0:T(8,128)(2,1)} async-done(((bf16[64,4096]{1,0:T(8,128)(2,1)}), bf16[64,1024]{1,0:T(8,128)(2,1)}) %reduce-scatter.8.cloned.1.call-update) | async-done | bytes 131088 | tf_op jit(solution)/shard_map/reduce_scatter | solution.py:173
  694.3 13.5 %all_gather.50 = bf16[64,4096]{1,0:T(8,128)(2,1)S(1)} all-gather(bf16[64,1024]{1,0:T(8,128)(2,1)S(1)} %broadcast_select_fusion.2), channel_id=1, replica_groups=mesh['section'=2,'blk'=16,'mp'=4] {'mp'}, dimensions={1}, use_global_device_ids=true | all-gather | bytes 655360 | tf_op jit(solution)/shard_map/all_gather | solution.py:118
  714.3 6.1 fusion.131
  720.6 7.0 collective-permute-done.33
  741.8 23.4 %all_gather.51 = bf16[1024,1,128]{2,0,1:T(8,128)(2,1)S(1)} all-gather(bf16[64,1,128]{2,0,1:T(8,128)(2,1)S(1)} %pad_maximum_fusion.2), channel_id=1, replica_groups=mesh['section'=2,'blk'=16,'mp'=4] {'blk'}, dimensions={0}, use_global_device_ids=true | all-gather | bytes 278528 | tf_op jit(solution)/shard_map/all_gather | solution.py:140
  800.3 20.3 %reduce-scatter.10.cloned.1.call-done = bf16[64,1024]{1,0:T(8,128)(2,1)} async-done(((bf16[64,4096]{1,0:T(8,128)(2,1)}), bf16[64,1024]{1,0:T(8,128)(2,1)}) %reduce-scatter.10.cloned.1.call-update) | async-done | bytes 131088 | tf_op jit(solution)/shard_map/reduce_scatter | solution.py:173
  824.8 13.4 %all_gather.52 = bf16[64,4096]{1,0:T(8,128)(2,1)S(1)} all-gather(bf16[64,1024]{1,0:T(8,128)(2,1)S(1)} %broadcast_select_fusion.1), channel_id=1, replica_groups=mesh['section'=2,'blk'=16,'mp'=4] {'mp'}, dimensions={1}, use_global_device_ids=true | all-gather | bytes 655360 | tf_op jit(solution)/shard_map/all_gather | solution.py:118
  851.0 7.0 collective-permute-done.49
  872.4 23.4 %all_gather.53 = bf16[1024,1,128]{2,0,1:T(8,128)(2,1)S(1)} all-gather(bf16[64,1,128]{2,0,1:T(8,128)(2,1)S(1)} %pad_maximum_fusion.3), channel_id=1, replica_groups=mesh['section'=2,'blk'=16,'mp'=4] {'blk'}, dimensions={0}, use_global_device_ids=true | all-gather | bytes 278528 | tf_op jit(solution)/shard_map/all_gather | solution.py:140
  930.4 21.5 %reduce-scatter.12.cloned.1.call-done = bf16[64,1024]{1,0:T(8,128)(2,1)} async-done(((bf16[64,4096]{1,0:T(8,128)(2,1)}), bf16[64,1024]{1,0:T(8,128)(2,1)}) %reduce-scatter.12.cloned.1.call-update) | async-done | bytes 131088 | tf_op jit(solution)/shard_map/reduce_scatter | solution.py:173
  958.5 13.2 %all_gather.54 = bf16[64,4096]{1,0:T(8,128)(2,1)S(1)} all-gather(bf16[64,1024]{1,0:T(8,128)(2,1)S(1)} %broadcast_select_fusion), channel_id=1, replica_groups=mesh['section'=2,'blk'=16,'mp'=4] {'mp'}, dimensions={1}, use_global_device_ids=true | all-gather | bytes 655360 | tf_op jit(solution)/shard_map/all_gather | solution.py:118
  984.4 7.0 collective-permute-done.65
  1005.6 23.4 %all_gather.55 = bf16[1024,1,128]{2,0,1:T(8,128)(2,1)S(1)} all-gather(bf16[64,1,128]{2,0,1:T(8,128)(2,1)S(1)} %pad_maximum_fusion.4), channel_id=1, replica_groups=mesh['section'=2,'blk'=16,'mp'=4] {'blk'}, dimensions={0}, use_global_device_ids=true | all-gather | bytes 278528 | tf_op jit(solution)/shard_map/all_gather | solution.py:140
  1061.8 20.8 %reduce-scatter.14.cloned.1.call-done = bf16[64,1024]{1,0:T(8,128)(2,1)} async-done(((bf16[64,4096]{1,0:T(8,128)(2,1)}), bf16[64,1024]{1,0:T(8,128)(2,1)}) %reduce-scatter.14.cloned.1.call-update) | async-done | bytes 131088 | tf_op jit(solution)/shard_map/reduce_scatter | solution.py:173
  (553 shorter events, 354.0 us)
Async XLA Ops:
  6.5 418.6 %all-gather.4.cloned.1.call-start = ((), (), s32[]{:S(2)}) async-start(), calls=%async_computation.5 | async-start | bytes 2228224 | tf_op jit(solution)/shard_map/all_gather | solution.py:87
  7.3 505.1 %all-gather.6.cloned.1.call-start = ((), (), s32[]{:S(2)}) async-start(), calls=%async_computation.6 | async-start | bytes 8912896 | tf_op jit(solution)/shard_map/all_gather | solution.py:86
  8.0 525.7 %all-gather.8.cloned.1.call-start = ((), (), s32[]{:S(2)}) async-start(), calls=%async_computation.7 | async-start | bytes 8912896 | tf_op jit(solution)/shard_map/all_gather | solution.py:88
  8.7 550.8 %reduce-scatter.6.cloned.1.call-start = ((), (), s32[]{:S(2)}) async-start(), calls=%async_computation.8 | async-start | bytes 655360 | tf_op jit(solution)/shard_map/reduce_scatter | solution.py:173
  467.0 29.6 %collective-permute-start.12 = (bf16[64,1,128]{2,0,1:T(8,128)(2,1)S(1)}, bf16[64,1,128]{2,0,1:T(8,128)(2,1)S(1)}, u32[]{:S(2)}, u32[]{:S(2)}) collective-permute-start(bf16[64,1,128]{2,0,1:T(8,128)(2,1)S(1)} %collective-permute-done.11), channel_id=1, source_target_pairs={{0,60},{4,0},{8,4},{12,8},{16,12},{20,16},{24,20},{28,24},{32,28},... | collective-permute-start | bytes 49160 | tf_op jit(solution)/shard_map/ppermute | solution.py:18
  473.2 26.1 %collective-permute-start.6 = (bf16[64,1,128]{2,0,1:T(8,128)(2,1)S(1)}, bf16[64,1,128]{2,0,1:T(8,128)(2,1)S(1)}, u32[]{:S(2)}, u32[]{:S(2)}) collective-permute-start(bf16[64,1,128]{2,0,1:T(8,128)(2,1)S(1)} %collective-permute-done.5), channel_id=1, source_target_pairs={{0,4},{4,8},{8,12},{12,16},{16,20},{20,24},{24,28},{28,32},{32,36}... | collective-permute-start | bytes 49160 | tf_op jit(solution)/shard_map/ppermute | solution.py:16
  539.6 151.5 %reduce-scatter.8.cloned.1.call-start = ((), (), s32[]{:S(2)}) async-start(), calls=%async_computation.9 | async-start | bytes 655360 | tf_op jit(solution)/shard_map/reduce_scatter | solution.py:173
  579.3 11.8 %collective-permute-start.16 = (bf16[64,1,128]{2,0,1:T(8,128)(2,1)S(1)}, bf16[64,1,128]{2,0,1:T(8,128)(2,1)S(1)}, u32[]{:S(2)}, u32[]{:S(2)}) collective-permute-start(bf16[64,1,128]{2,0,1:T(8,128)(2,1)S(1)} %fusion.285), channel_id=1, source_target_pairs={{0,4},{4,8},{8,12},{12,16},{16,20},{20,24},{24,28},{28,32},{32,36}... | collective-permute-start | bytes 49160 | tf_op jit(solution)/shard_map/ppermute | solution.py:16
  580.9 17.6 %collective-permute-start.24 = (bf16[64,1,128]{2,0,1:T(8,128)(2,1)S(1)}, bf16[64,1,128]{2,0,1:T(8,128)(2,1)S(1)}, u32[]{:S(2)}, u32[]{:S(2)}) collective-permute-start(bf16[64,1,128]{2,0,1:T(8,128)(2,1)S(1)} %fusion.285), channel_id=1, source_target_pairs={{0,60},{4,0},{8,4},{12,8},{16,12},{20,16},{24,20},{28,24},{32,28},... | collective-permute-start | bytes 49160 | tf_op jit(solution)/shard_map/ppermute | solution.py:18
  605.6 30.3 %collective-permute-start.26 = (bf16[64,1,128]{2,0,1:T(8,128)(2,1)S(1)}, bf16[64,1,128]{2,0,1:T(8,128)(2,1)S(1)}, u32[]{:S(2)}, u32[]{:S(2)}) collective-permute-start(bf16[64,1,128]{2,0,1:T(8,128)(2,1)S(1)} %collective-permute-done.25), channel_id=1, source_target_pairs={{0,60},{4,0},{8,4},{12,8},{16,12},{20,16},{24,20},{28,24},{32,28},... | collective-permute-start | bytes 49160 | tf_op jit(solution)/shard_map/ppermute | solution.py:18
  612.5 26.1 %collective-permute-start.20 = (bf16[64,1,128]{2,0,1:T(8,128)(2,1)S(1)}, bf16[64,1,128]{2,0,1:T(8,128)(2,1)S(1)}, u32[]{:S(2)}, u32[]{:S(2)}) collective-permute-start(bf16[64,1,128]{2,0,1:T(8,128)(2,1)S(1)} %collective-permute-done.19), channel_id=1, source_target_pairs={{0,4},{4,8},{8,12},{12,16},{16,20},{20,24},{24,28},{28,32},{32,36}... | collective-permute-start | bytes 49160 | tf_op jit(solution)/shard_map/ppermute | solution.py:16
  669.5 151.2 %reduce-scatter.10.cloned.1.call-start = ((), (), s32[]{:S(2)}) async-start(), calls=%async_computation.10 | async-start | bytes 655360 | tf_op jit(solution)/shard_map/reduce_scatter | solution.py:173
  708.9 11.7 %collective-permute-start.32 = (bf16[64,1,128]{2,0,1:T(8,128)(2,1)S(1)}, bf16[64,1,128]{2,0,1:T(8,128)(2,1)S(1)}, u32[]{:S(2)}, u32[]{:S(2)}) collective-permute-start(bf16[64,1,128]{2,0,1:T(8,128)(2,1)S(1)} %fusion.286), channel_id=1, source_target_pairs={{0,4},{4,8},{8,12},{12,16},{16,20},{20,24},{24,28},{28,32},{32,36}... | collective-permute-start | bytes 49160 | tf_op jit(solution)/shard_map/ppermute | solution.py:16
  710.5 17.4 %collective-permute-start.40 = (bf16[64,1,128]{2,0,1:T(8,128)(2,1)S(1)}, bf16[64,1,128]{2,0,1:T(8,128)(2,1)S(1)}, u32[]{:S(2)}, u32[]{:S(2)}) collective-permute-start(bf16[64,1,128]{2,0,1:T(8,128)(2,1)S(1)} %fusion.286), channel_id=1, source_target_pairs={{0,60},{4,0},{8,4},{12,8},{16,12},{20,16},{24,20},{28,24},{32,28},... | collective-permute-start | bytes 49160 | tf_op jit(solution)/shard_map/ppermute | solution.py:18
  734.8 30.3 %collective-permute-start.42 = (bf16[64,1,128]{2,0,1:T(8,128)(2,1)S(1)}, bf16[64,1,128]{2,0,1:T(8,128)(2,1)S(1)}, u32[]{:S(2)}, u32[]{:S(2)}) collective-permute-start(bf16[64,1,128]{2,0,1:T(8,128)(2,1)S(1)} %collective-permute-done.41), channel_id=1, source_target_pairs={{0,60},{4,0},{8,4},{12,8},{16,12},{20,16},{24,20},{28,24},{32,28},... | collective-permute-start | bytes 49160 | tf_op jit(solution)/shard_map/ppermute | solution.py:18
  741.8 26.1 %collective-permute-start.36 = (bf16[64,1,128]{2,0,1:T(8,128)(2,1)S(1)}, bf16[64,1,128]{2,0,1:T(8,128)(2,1)S(1)}, u32[]{:S(2)}, u32[]{:S(2)}) collective-permute-start(bf16[64,1,128]{2,0,1:T(8,128)(2,1)S(1)} %collective-permute-done.35), channel_id=1, source_target_pairs={{0,4},{4,8},{8,12},{12,16},{16,20},{20,24},{24,28},{28,32},{32,36}... | collective-permute-start | bytes 49160 | tf_op jit(solution)/shard_map/ppermute | solution.py:16
  799.0 152.8 %reduce-scatter.12.cloned.1.call-start = ((), (), s32[]{:S(2)}) async-start(), calls=%async_computation.11 | async-start | bytes 655360 | tf_op jit(solution)/shard_map/reduce_scatter | solution.py:173
  840.8 17.7 %collective-permute-start.56 = (bf16[64,1,128]{2,0,1:T(8,128)(2,1)S(1)}, bf16[64,1,128]{2,0,1:T(8,128)(2,1)S(1)}, u32[]{:S(2)}, u32[]{:S(2)}) collective-permute-start(bf16[64,1,128]{2,0,1:T(8,128)(2,1)S(1)} %fusion.287), channel_id=1, source_target_pairs={{0,60},{4,0},{8,4},{12,8},{16,12},{20,16},{24,20},{28,24},{32,28},... | collective-permute-start | bytes 49160 | tf_op jit(solution)/shard_map/ppermute | solution.py:18
  865.4 30.3 %collective-permute-start.58 = (bf16[64,1,128]{2,0,1:T(8,128)(2,1)S(1)}, bf16[64,1,128]{2,0,1:T(8,128)(2,1)S(1)}, u32[]{:S(2)}, u32[]{:S(2)}) collective-permute-start(bf16[64,1,128]{2,0,1:T(8,128)(2,1)S(1)} %collective-permute-done.57), channel_id=1, source_target_pairs={{0,60},{4,0},{8,4},{12,8},{16,12},{20,16},{24,20},{28,24},{32,28},... | collective-permute-start | bytes 49160 | tf_op jit(solution)/shard_map/ppermute | solution.py:18
  872.4 26.1 %collective-permute-start.52 = (bf16[64,1,128]{2,0,1:T(8,128)(2,1)S(1)}, bf16[64,1,128]{2,0,1:T(8,128)(2,1)S(1)}, u32[]{:S(2)}, u32[]{:S(2)}) collective-permute-start(bf16[64,1,128]{2,0,1:T(8,128)(2,1)S(1)} %collective-permute-done.51), channel_id=1, source_target_pairs={{0,4},{4,8},{8,12},{12,16},{16,20},{20,24},{24,28},{28,32},{32,36}... | collective-permute-start | bytes 49160 | tf_op jit(solution)/shard_map/ppermute | solution.py:16
  930.3 152.2 %reduce-scatter.14.cloned.1.call-start = ((), (), s32[]{:S(2)}) async-start(), calls=%async_computation.12 | async-start | bytes 655360 | tf_op jit(solution)/shard_map/reduce_scatter | solution.py:173
  974.3 17.4 %collective-permute-start.72 = (bf16[64,1,128]{2,0,1:T(8,128)(2,1)S(1)}, bf16[64,1,128]{2,0,1:T(8,128)(2,1)S(1)}, u32[]{:S(2)}, u32[]{:S(2)}) collective-permute-start(bf16[64,1,128]{2,0,1:T(8,128)(2,1)S(1)} %fusion.288), channel_id=1, source_target_pairs={{0,60},{4,0},{8,4},{12,8},{16,12},{20,16},{24,20},{28,24},{32,28},... | collective-permute-start | bytes 49160 | tf_op jit(solution)/shard_map/ppermute | solution.py:18
  998.6 30.4 %collective-permute-start.74 = (bf16[64,1,128]{2,0,1:T(8,128)(2,1)S(1)}, bf16[64,1,128]{2,0,1:T(8,128)(2,1)S(1)}, u32[]{:S(2)}, u32[]{:S(2)}) collective-permute-start(bf16[64,1,128]{2,0,1:T(8,128)(2,1)S(1)} %collective-permute-done.73), channel_id=1, source_target_pairs={{0,60},{4,0},{8,4},{12,8},{16,12},{20,16},{24,20},{28,24},{32,28},... | collective-permute-start | bytes 49160 | tf_op jit(solution)/shard_map/ppermute | solution.py:18
  1005.6 26.1 %collective-permute-start.68 = (bf16[64,1,128]{2,0,1:T(8,128)(2,1)S(1)}, bf16[64,1,128]{2,0,1:T(8,128)(2,1)S(1)}, u32[]{:S(2)}, u32[]{:S(2)}) collective-permute-start(bf16[64,1,128]{2,0,1:T(8,128)(2,1)S(1)} %collective-permute-done.67), channel_id=1, source_target_pairs={{0,4},{4,8},{8,12},{12,16},{16,20},{20,24},{24,28},{28,32},{32,36}... | collective-permute-start | bytes 49160 | tf_op jit(solution)/shard_map/ppermute | solution.py:16
  (139 other events, 6257.8 us)
Sparse Core Ops, SparseCore 0:
  9.5 47.4 all-gather.3
  59.1 73.9 all-gather.5
  135.3 83.4 all-gather.7
  539.7 19.7 reduce-scatter.5
  669.6 21.3 reduce-scatter.7
  799.2 21.4 reduce-scatter.9
  930.5 21.3 reduce-scatter.11
  1061.1 21.3 reduce-scatter.13
